TPU v7x, 256 devices: a whole 4x4x8 slice. The times are simulated.
256 devices in a mesh: side: 2 (over x_hi), row: 32 (over y, z), col: 4 (over x_lo, core).
Axes of the slice: x: 4 (x_hi: 2, x_lo: 2; x = x_hi * 2 + x_lo), y: 4, z: 8, core: 2. Of those that a mesh axis runs over, the one named last changes fastest.
Arguments:
- old_vectors: bfloat16 [2, 32768, 16384], P('side', 'row', 'col'), may hold values from -6 to 6
- reflectors: bfloat16 [2, 2, 32768, 512], P('side', None, 'row', 'col'), may hold values from -0.0625 to 0.0625
- triangles: float32 [2, 2, 512, 512], P('side'), may hold values from -0.25 to 0.25
- pole_sq: float32 [32768], replicated, may hold values from 1 to 65536, as said below
- coupling: float32 [32768], replicated, may hold values from -1 to 1
- deflated: int32 [32768], replicated, may hold values 0 or 1
- pole_order: int32 [32768], replicated, may hold values from 0 to 32767, each once
- anchors: int32 [1024], replicated, may hold values from 0 to 32766, as said below
- root_fraction: float32 [1024], replicated, may hold values from 0.2 to 0.8
Outputs:
- vectors: bfloat16 [2, 1024, 32768], P('side', 'col', 'row')
Inputs may be any that keep to these rules, and one draw needn't show every extreme that they name: `pole_sq`: strictly increasing; successive entries differ by 0.5 or more. `anchors`: distinct entries.
All inputs are finite; a program needn't handle non-finite values.
Results may differ from a plain program's by a relative error of at most 0.014.
Values may be sent and summed in bfloat16 or wider, within the bound.
A program may use at most 128 MiB of HBM per device.

v0:
```python
import jax
import jax.numpy as jnp
from jax import lax
from jax.sharding import PartitionSpec as P


def secular_columns(col_sq, col_coupling, col_live, weight, anchor_sq, pole_gap, root_fraction):
    denom = col_sq[:, None] - anchor_sq[None, :] - root_fraction[None, :] * pole_gap[None, :]
    return (col_live * col_coupling * weight)[:, None] / denom


def per_device(
    old_vectors,
    reflectors,
    triangles,
    pole_sq,
    coupling,
    deflated,
    pole_order,
    anchors,
    root_fraction,
):
    side_index = lax.axis_index("side")
    row_index = lax.axis_index("row")
    col_index = lax.axis_index("col")
    half_rows = lax.axis_size("row") // 2
    col_count = lax.axis_size("col")
    old_block = old_vectors[0]
    col_width = old_block.shape[1]
    order_size = pole_sq.shape[0]
    triplets = anchors.shape[0]
    local_triplets = triplets // col_count
    first_column = row_index // half_rows * (order_size // 2) + col_index * col_width
    columns = first_column + jnp.arange(col_width, dtype=jnp.int32)
    position = (
        jnp.zeros((order_size,), jnp.int32)
        .at[pole_order]
        .set(jnp.arange(order_size, dtype=jnp.int32))
    )
    sorted_pos = lax.dynamic_slice_in_dim(position, first_column, col_width)
    col_sq = pole_sq[sorted_pos]
    col_coupling = coupling[sorted_pos]
    col_live = (1 - deflated[sorted_pos]).astype(jnp.float32)
    weight = jnp.where(side_index == 0, jnp.ones_like(col_sq), jnp.sqrt(col_sq))
    anchor_sq = pole_sq[anchors]
    pole_gap = pole_sq[anchors + 1] - anchor_sq
    dead_triplet = deflated[anchors] == 1
    target = pole_order[anchors]
    secular = secular_columns(
        col_sq, col_coupling, col_live, weight, anchor_sq, pole_gap, root_fraction
    )
    onehot = (columns[:, None] == target[None, :]).astype(jnp.float32)
    mixing = jnp.where(dead_triplet[None, :], onehot, secular).astype(jnp.bfloat16)
    share_size = col_width // half_rows
    slice_part = lax.dynamic_slice_in_dim(
        secular, row_index % half_rows * share_size, share_size, 0
    )
    squares = lax.psum(jnp.sum(slice_part * slice_part, axis=0), ("row", "col"))
    col_scale = jnp.where(dead_triplet, jnp.ones_like(squares), 1.0 / jnp.sqrt(squares + 1e-06))
    merged = lax.psum_scatter(
        jnp.einsum("ck,rc->kr", mixing, old_block, preferred_element_type=jnp.float32).astype(
            jnp.bfloat16
        ),
        "col",
        scatter_dimension=0,
        tiled=True,
    ).astype(jnp.float32)
    my_scale = lax.dynamic_slice_in_dim(col_scale, col_index * local_triplets, local_triplets)
    vectors = merged * my_scale[:, None]
    panel_local = reflectors[0]
    panels = panel_local.shape[0]
    upper_tri = jnp.triu(triangles[0])
    highest = lax.Precision.HIGHEST
    for panel_index in reversed(range(panels)):
        panel_rows = panel_local[panel_index]
        current = vectors
        current_low = current.astype(jnp.bfloat16)
        projected = jnp.dot(
            current_low,
            lax.all_gather(panel_rows, "col", axis=1, tiled=True),
            preferred_element_type=jnp.float32,
        )
        projected = lax.psum(projected.astype(jnp.bfloat16), "row").astype(jnp.float32)
        coefficients = jnp.dot(projected, upper_tri[panel_index].T, precision=highest).astype(
            jnp.bfloat16
        )
        vectors = current - jnp.dot(
            coefficients,
            lax.all_gather(panel_rows, "col", axis=1, tiled=True).T,
            preferred_element_type=jnp.float32,
        )
    return vectors.astype(jnp.bfloat16)[None]


def solution(mesh):
    in_specs = (
        P("side", "row", "col"),
        P("side", None, "row", "col"),
        P("side", None, None, None),
        P(),
        P(),
        P(),
        P(),
        P(),
        P(),
    )
    out_specs = P("side", "col", "row")
    return jax.shard_map(
        per_device, mesh=mesh, in_specs=in_specs, out_specs=out_specs, check_vma=False
    )
```

profile of v0, /device:TPU:2, one launch (start us, length us, event | category | flops | bytes accessed | tf_op | source)
XLA Modules:
  0.0 883.1 jit_solution(16158088718118967877)
XLA Ops:
  6.5 0.0 copy-start
  6.5 0.0 all-gather.5.cloned.1.call-start
  6.5 1.9 fusion.23
  8.4 0.0 all-gather.5.cloned.1.call-update
  8.4 0.0 reduce-scatter.2.cloned.1.call-start
  8.5 0.9 compare_select_fusion
  9.5 120.1 %scatter_custom_fusion = s32[32768]{0:T(1024)S(1)} fusion(s32[32768]{0:T(1024)S(1)} %compare_select_fusion, s32[32768]{0:T(1024)S(1)} %iota.24, s32[]{:T(128)} %constant.23.clone.1), kind=kCustom, calls=%fused_computation.38 | custom fusion | bytes 131076 | tf_op jit(solution)/shard_map/scatter | solution.py:38
  129.6 0.0 copy-start.4
  129.6 0.0 copy-start.1
  129.6 19.5 %gather_fusion.2 = s32[4096]{0:T(1024)S(1)} fusion(s32[32768]{0:T(1024)} %param.14, s32[4096]{0:T(1024)S(1)} %fusion.20), kind=kCustom, calls=%fused_computation.2 | custom fusion | bytes 49152 | tf_op jit(solution)/shard_map/gather | solution.py:43
  149.2 0.0 copy-done
  149.2 0.0 copy-start.3
  149.2 0.0 copy-start.2
  149.2 23.0 %gather_fusion.4 = f32[4096]{0:T(1024)S(1)} fusion(f32[32768]{0:T(1024)S(1)} %copy-done, s32[4096]{0:T(1024)S(1)} %fusion.20), kind=kCustom, calls=%fused_computation.4 | custom fusion | bytes 49152 | tf_op jit(solution)/shard_map/gather | solution.py:41
  172.2 0.0 copy-done.4
  172.3 0.0 copy-start.5
  172.3 6.2 gather_fusion.5
  178.4 0.0 copy-done.1
  178.4 6.2 gather_fusion
  184.6 0.0 copy-done.3
  184.6 6.2 gather_fusion.1
  190.8 0.0 copy-done.2
  190.8 23.0 %gather_fusion.3 = f32[4096]{0:T(1024)S(1)} fusion(f32[32768]{0:T(1024)S(1)} %copy-done.2, s32[4096]{0:T(1024)S(1)} %fusion.20), kind=kCustom, calls=%fused_computation.3 | custom fusion | bytes 49152 | tf_op jit(solution)/shard_map/gather | solution.py:42
  213.8 6.2 gather_fusion.6
  220.0 0.0 copy-done.5
  220.0 6.5 subtract_divide_fusion
  226.5 1.3 multiply_reduce_fusion
  227.8 278.5 %psum.21 = f32[1024]{0:T(1024)S(1)} all-reduce(f32[1024]{0:T(1024)S(1)} %multiply_reduce_fusion), channel_id=1, replica_groups=mesh['side'=2,'row'=32,'col'=4] {'row','col'}, use_global_device_ids=true, to_apply=%region_3.4 | all-reduce | flops 1024 | bytes 8192 | tf_op jit(solution)/shard_map/psum | solution.py:58
  506.3 15.3 %fusion.5 = bf16[1024,1024]{1,0:T(8,128)(2,1)} fusion(bf16[1,1024,4096]{2,1,0:T(8,128)(2,1)} %param.9, s32[1024]{0:T(1024)S(1)} %gather_fusion.1, s32[4096]{0:T(1024)S(1)} %iota_add_fusion, pred[1024]{0:T(1024)(128)(4,1)S(1)} %get-tuple-element.6, f32[1024]{0:T(1024)S(1)} %subtract_multiply_fusion, f32[1024]{0:T(1024)S(1)} %gather_fusion.5, ...), kind=kOutput, calls=%fused_computation.16 | convolution fusion | flops 8620343296 | bytes 10548224 | tf_op jit(solution)/shard_map/ck,rc->kr/dot_general | solution.py:61
  521.7 0.0 reduce-scatter.2.cloned.1.call-update
  521.7 0.0 all-reduce.3.cloned.1.call-start
  521.8 0.1 dynamic_slice.11
  521.8 0.0 all-gather.5.cloned.1.call-done
  521.8 28.4 %reduce-scatter.2.cloned.1.call-done = bf16[256,1024]{1,0:T(8,128)(2,1)} async-done(((bf16[1024,1024]{1,0:T(8,128)(2,1)}), bf16[256,1024]{1,0:T(8,128)(2,1)}) %reduce-scatter.2.cloned.1.call-update) | async-done | bytes 524304 | tf_op jit(solution)/shard_map/reduce_scatter | solution.py:60
  550.3 2.6 convolution_convert_fusion.3
  552.9 0.0 all-reduce.3.cloned.1.call-update
  552.9 0.0 all-gather.7.cloned.1.call-start
  552.9 0.5 all-gather.7.cloned.1.call-update
  553.5 0.3 all-reduce.5.cloned.1.call-start
  553.7 0.2 iota_compare_fusion
  554.0 2.0 bitcast_select_fusion
  555.9 145.1 %all-reduce.3.cloned.1.call-done = bf16[256,512]{1,0:T(8,128)(2,1)} async-done(((bf16[256,512]{1,0:T(8,128)(2,1)}), bf16[256,512]{1,0:T(8,128)(2,1)}) %all-reduce.3.cloned.1.call-update) | async-done | bytes 262160 | tf_op jit(solution)/shard_map/psum | solution.py:83
  701.0 1.6 convolution_convert_fusion.2
  702.6 1.8 convolution_subtract_fusion.1
  704.5 18.7 %all-gather.7.cloned.1.call-done = bf16[1,1,1024,512]{3,2,1,0:T(8,128)(2,1)} async-done(((bf16[1,1,1024,128]{3,2,1,0:T(8,128)(2,1)}), bf16[1,1,1024,512]{3,2,1,0:T(8,128)(2,1)}) %all-gather.7.cloned.1.call-update) | async-done | bytes 1048592 | tf_op jit(solution)/shard_map/all_gather | solution.py:80
  723.1 2.4 convolution_convert_fusion.1
  725.5 0.0 all-reduce.5.cloned.1.call-update
  725.5 146.9 %all-reduce.5.cloned.1.call-done = bf16[256,512]{1,0:T(8,128)(2,1)} async-done(((bf16[256,512]{1,0:T(8,128)(2,1)}), bf16[256,512]{1,0:T(8,128)(2,1)}) %all-reduce.5.cloned.1.call-update) | async-done | bytes 262160 | tf_op jit(solution)/shard_map/psum | solution.py:83
  872.4 1.6 convolution_convert_fusion
  874.1 2.5 fusion.9
  (8 shorter events, 0.1 us)
Async XLA Ops:
  6.5 142.6 %copy-start = (f32[32768]{0:T(1024)S(1)}, f32[32768]{0:T(1024)}, u32[]{:S(2)}) copy-start(f32[32768]{0:T(1024)} %param.12) | copy-start | bytes 393220
  6.5 515.3 %all-gather.5.cloned.1.call-start = ((), (), s32[]{:S(2)}) async-start(), calls=%async_computation.4 | async-start | bytes 1310720 | tf_op jit(solution)/shard_map/all_gather | solution.py:80
  8.4 541.8 %reduce-scatter.2.cloned.1.call-start = ((), (), s32[]{:S(2)}) async-start(), calls=%async_computation.1 | async-start | bytes 2621440 | tf_op jit(solution)/shard_map/reduce_scatter | solution.py:60
  129.6 42.6 %copy-start.4 = (s32[1024]{0:T(1024)S(1)}, s32[1024]{0:T(1024)}, u32[]{:S(2)}) copy-start(s32[1024]{0:T(1024)} %param.16) | copy-start | bytes 12292
  129.6 48.8 %copy-start.1 = (s32[32768]{0:T(1024)S(1)}, s32[32768]{0:T(1024)}, u32[]{:S(2)}) copy-start(s32[32768]{0:T(1024)} %param.14) | copy-start | bytes 393220
  149.2 35.4 %copy-start.3 = (s32[32768]{0:T(1024)S(1)}, s32[32768]{0:T(1024)}, u32[]{:S(2)}) copy-start(s32[32768]{0:T(1024)} %param.15) | copy-start | bytes 393220
  149.2 41.6 %copy-start.2 = (f32[32768]{0:T(1024)S(1)}, f32[32768]{0:T(1024)}, u32[]{:S(2)}) copy-start(f32[32768]{0:T(1024)} %param.13) | copy-start | bytes 393220
  172.3 47.7 %copy-start.5 = (f32[1024]{0:T(1024)S(1)}, f32[1024]{0:T(1024)}, u32[]{:S(2)}) copy-start(f32[1024]{0:T(1024)} %param.17) | copy-start | bytes 12292
  521.7 179.3 %all-reduce.3.cloned.1.call-start = ((), (), s32[]{:S(2)}) async-start(), calls=%async_computation.2 | async-start | bytes 524288 | tf_op jit(solution)/shard_map/psum | solution.py:83
  552.9 170.3 %all-gather.7.cloned.1.call-start = ((), (), s32[]{:S(2)}) async-start(), calls=%async_computation.5 | async-start | bytes 1310720 | tf_op jit(solution)/shard_map/all_gather | solution.py:80
  553.5 319.0 %all-reduce.5.cloned.1.call-start = ((), (), s32[]{:S(2)}) async-start(), calls=%async_computation.3 | async-start | bytes 524288 | tf_op jit(solution)/shard_map/psum | solution.py:83
Sparse Core Ops, SparseCore 0:
  9.2 26.2 all-gather.4
  521.8 28.4 reduce-scatter.1
  554.1 146.8 all-reduce.2
  702.8 20.2 all-gather.6
  726.8 145.5 all-reduce.4
where the time goes:
time: 884 us; the launch traced here: 883 us
  waiting for transfers between devices  340 us (38%)
  blocking collectives  278 us (31%)
  local copies, waits for them, and re-layouts  212 us (24%)
  matrix products  27.8 us (3%)
  between operations  13.4 us (2%)
  other arithmetic  10.9 us (1%)
    psum x2, waiting for transfers between devices, per_device(): lax.psum(projected.astype(jnp.bfloat16), 'row').astype(jnp.float32)  292 us
    psum x1, blocking collectives, per_device(): squares = lax.psum(jnp.sum(slice_part * slice_part, axis=0), ('row', 'col'))  278 us
    scatter x1, local copies, waits for them, and re-layouts, per_device(): position = jnp.zeros((order_size,), jnp.int32).at[pole_order].set(jnp.ara...  120 us
    reduce_scatter x1, waiting for transfers between devices, per_device(): lax.psum_scatter(jnp.einsum('ck,rc->kr', mixing, old_block, preferred_ele...  28.4 us
    gather x1, local copies, waits for them, and re-layouts, per_device(): col_sq = pole_sq[sorted_pos]  23 us
    gather x1, local copies, waits for them, and re-layouts, per_device(): col_coupling = coupling[sorted_pos]  23 us
    gather x1, local copies, waits for them, and re-layouts, per_device(): col_live = (1 - deflated[sorted_pos]).astype(jnp.float32)  19.5 us
    all_gather x2, waiting for transfers between devices, per_device(): lax.all_gather(panel_rows, 'col', axis=1, tiled=True)  18.7 us
  transfers between devices with their start and end apart: 5, of which 4 were waited for; matrix products, arithmetic and copies ran while one was open for 27% of the time, Pallas kernels for 0%

commit v1 on v0

--- a/solution.py
+++ b/solution.py
@@ -55,7 +55,7 @@
     slice_part = lax.dynamic_slice_in_dim(
         secular, row_index % half_rows * share_size, share_size, 0
     )
-    squares = lax.psum(jnp.sum(slice_part * slice_part, axis=0), ("row", "col"))
+    squares = lax.psum(lax.psum(jnp.sum(slice_part * slice_part, axis=0), "row"), "col")
     col_scale = jnp.where(dead_triplet, jnp.ones_like(squares), 1.0 / jnp.sqrt(squares + 1e-06))
     merged = lax.psum_scatter(
         jnp.einsum("ck,rc->kr", mixing, old_block, preferred_element_type=jnp.float32).astype(

time: 884 us -> 683 us (0.77)
  blocking collectives: 278 us -> 83.8 us
    psum x1 -> x2, blocking collectives: 278 us -> 83.8 us  [the longest x1 77.9 us: per_device(): lax.psum(jnp.sum(slice_part * slice_part, axis=0), 'row')]
  transfers between devices with their start and end apart: 5 -> 5, of which waited for: 4 -> 4; matrix products, arithmetic and copies ran while one was open for 27% -> 35% of each run, Pallas kernels for 0% -> 0%
where the time goes in v1:
time: 683 us; the launch traced here: 682 us
  waiting for transfers between devices  334 us (49%)
  local copies, waits for them, and re-layouts  212 us (31%)
  blocking collectives  83.8 us (12%)
  matrix products  27.8 us (4%)
  between operations  13.4 us (2%)
  other arithmetic  10.9 us (2%)
    psum x2, waiting for transfers between devices, per_device(): lax.psum(projected.astype(jnp.bfloat16), 'row').astype(jnp.float32)  292 us
    scatter x1, local copies, waits for them, and re-layouts, per_device(): position = jnp.zeros((order_size,), jnp.int32).at[pole_order].set(jnp.ara...  120 us
    psum x1, blocking collectives, per_device(): lax.psum(jnp.sum(slice_part * slice_part, axis=0), 'row')  77.9 us
    gather x1, local copies, waits for them, and re-layouts, per_device(): col_sq = pole_sq[sorted_pos]  23 us
    gather x1, local copies, waits for them, and re-layouts, per_device(): col_coupling = coupling[sorted_pos]  23 us
    reduce_scatter x1, waiting for transfers between devices, per_device(): lax.psum_scatter(jnp.einsum('ck,rc->kr', mixing, old_block, preferred_ele...  22.6 us
    gather x1, local copies, waits for them, and re-layouts, per_device(): col_live = (1 - deflated[sorted_pos]).astype(jnp.float32)  19.5 us
    all_gather x2, waiting for transfers between devices, per_device(): lax.all_gather(panel_rows, 'col', axis=1, tiled=True)  18.7 us
  transfers between devices with their start and end apart: 5, of which 4 were waited for; matrix products, arithmetic and copies ran while one was open for 35% of the time, Pallas kernels for 0%

profile of v1, /device:TPU:2, one launch (start us, length us, event | category | flops | bytes accessed | tf_op | source)
XLA Modules:
  0.0 682.5 jit_solution(9622185338462220297)
XLA Ops:
  6.5 0.0 copy-start
  6.5 0.0 all-gather.5.cloned.1.call-start
  6.5 1.9 fusion.23
  8.4 0.0 all-gather.5.cloned.1.call-update
  8.4 0.0 reduce-scatter.2.cloned.1.call-start
  8.5 0.9 compare_select_fusion
  9.5 120.1 %scatter_custom_fusion = s32[32768]{0:T(1024)S(1)} fusion(s32[32768]{0:T(1024)S(1)} %compare_select_fusion, s32[32768]{0:T(1024)S(1)} %iota.24, s32[]{:T(128)} %constant.23.clone.1), kind=kCustom, calls=%fused_computation.38 | custom fusion | bytes 131076 | tf_op jit(solution)/shard_map/scatter | solution.py:38
  129.6 0.0 copy-start.4
  129.6 0.0 copy-start.1
  129.6 19.5 %gather_fusion.2 = s32[4096]{0:T(1024)S(1)} fusion(s32[32768]{0:T(1024)} %param.14, s32[4096]{0:T(1024)S(1)} %fusion.20), kind=kCustom, calls=%fused_computation.2 | custom fusion | bytes 49152 | tf_op jit(solution)/shard_map/gather | solution.py:43
  149.2 0.0 copy-done
  149.2 0.0 copy-start.3
  149.2 0.0 copy-start.2
  149.2 23.0 %gather_fusion.4 = f32[4096]{0:T(1024)S(1)} fusion(f32[32768]{0:T(1024)S(1)} %copy-done, s32[4096]{0:T(1024)S(1)} %fusion.20), kind=kCustom, calls=%fused_computation.4 | custom fusion | bytes 49152 | tf_op jit(solution)/shard_map/gather | solution.py:41
  172.2 0.0 copy-done.4
  172.3 0.0 copy-start.5
  172.3 6.2 gather_fusion.5
  178.4 0.0 copy-done.1
  178.4 6.2 gather_fusion
  184.6 0.0 copy-done.3
  184.6 6.2 gather_fusion.1
  190.8 0.0 copy-done.2
  190.8 23.0 %gather_fusion.3 = f32[4096]{0:T(1024)S(1)} fusion(f32[32768]{0:T(1024)S(1)} %copy-done.2, s32[4096]{0:T(1024)S(1)} %fusion.20), kind=kCustom, calls=%fused_computation.3 | custom fusion | bytes 49152 | tf_op jit(solution)/shard_map/gather | solution.py:42
  213.8 6.2 gather_fusion.6
  220.0 0.0 copy-done.5
  220.0 6.4 subtract_divide_fusion
  226.5 1.3 multiply_reduce_fusion
  227.8 77.9 %psum.28 = f32[1024]{0:T(1024)S(1)} all-reduce(f32[1024]{0:T(1024)S(1)} %multiply_reduce_fusion), channel_id=1, replica_groups=mesh['side'=2,'row'=32,'col'=4] {'row'}, use_global_device_ids=true, to_apply=%region_3.4 | all-reduce | flops 1024 | bytes 8192 | tf_op jit(solution)/shard_map/psum | solution.py:58
  305.7 5.9 psum.29
  311.7 15.3 %fusion.5 = bf16[1024,1024]{1,0:T(8,128)(2,1)} fusion(bf16[1,1024,4096]{2,1,0:T(8,128)(2,1)} %param.9, s32[1024]{0:T(1024)S(1)} %gather_fusion.1, s32[4096]{0:T(1024)S(1)} %iota_add_fusion, pred[1024]{0:T(1024)(128)(4,1)S(1)} %get-tuple-element.6, f32[1024]{0:T(1024)S(1)} %subtract_multiply_fusion, f32[1024]{0:T(1024)S(1)} %gather_fusion.5, ...), kind=kOutput, calls=%fused_computation.16 | convolution fusion | flops 8620343296 | bytes 10548224 | tf_op jit(solution)/shard_map/ck,rc->kr/dot_general | solution.py:61
  327.0 0.0 reduce-scatter.2.cloned.1.call-update
  327.0 0.0 all-reduce.3.cloned.1.call-start
  327.1 0.1 dynamic_slice.11
  327.1 0.0 all-gather.5.cloned.1.call-done
  327.1 22.6 %reduce-scatter.2.cloned.1.call-done = bf16[256,1024]{1,0:T(8,128)(2,1)} async-done(((bf16[1024,1024]{1,0:T(8,128)(2,1)}), bf16[256,1024]{1,0:T(8,128)(2,1)}) %reduce-scatter.2.cloned.1.call-update) | async-done | bytes 524304 | tf_op jit(solution)/shard_map/reduce_scatter | solution.py:60
  349.7 2.6 convolution_convert_fusion.3
  352.3 0.0 all-reduce.3.cloned.1.call-update
  352.3 0.0 all-gather.7.cloned.1.call-start
  352.4 0.5 all-gather.7.cloned.1.call-update
  352.9 0.3 all-reduce.5.cloned.1.call-start
  353.2 0.2 iota_compare_fusion
  353.4 2.0 bitcast_select_fusion
  355.3 145.0 %all-reduce.3.cloned.1.call-done = bf16[256,512]{1,0:T(8,128)(2,1)} async-done(((bf16[256,512]{1,0:T(8,128)(2,1)}), bf16[256,512]{1,0:T(8,128)(2,1)}) %all-reduce.3.cloned.1.call-update) | async-done | bytes 262160 | tf_op jit(solution)/shard_map/psum | solution.py:83
  500.4 1.6 convolution_convert_fusion.2
  502.0 1.8 convolution_subtract_fusion.1
  503.9 18.7 %all-gather.7.cloned.1.call-done = bf16[1,1,1024,512]{3,2,1,0:T(8,128)(2,1)} async-done(((bf16[1,1,1024,128]{3,2,1,0:T(8,128)(2,1)}), bf16[1,1,1024,512]{3,2,1,0:T(8,128)(2,1)}) %all-gather.7.cloned.1.call-update) | async-done | bytes 1048592 | tf_op jit(solution)/shard_map/all_gather | solution.py:80
  522.5 2.4 convolution_convert_fusion.1
  524.9 0.0 all-reduce.5.cloned.1.call-update
  524.9 146.9 %all-reduce.5.cloned.1.call-done = bf16[256,512]{1,0:T(8,128)(2,1)} async-done(((bf16[256,512]{1,0:T(8,128)(2,1)}), bf16[256,512]{1,0:T(8,128)(2,1)}) %all-reduce.5.cloned.1.call-update) | async-done | bytes 262160 | tf_op jit(solution)/shard_map/psum | solution.py:83
  671.8 1.6 convolution_convert_fusion
  673.4 2.5 fusion.9
  (8 shorter events, 0.1 us)
Async XLA Ops:
  6.5 142.6 %copy-start = (f32[32768]{0:T(1024)S(1)}, f32[32768]{0:T(1024)}, u32[]{:S(2)}) copy-start(f32[32768]{0:T(1024)} %param.12) | copy-start | bytes 393220
  6.5 320.6 %all-gather.5.cloned.1.call-start = ((), (), s32[]{:S(2)}) async-start(), calls=%async_computation.4 | async-start | bytes 1310720 | tf_op jit(solution)/shard_map/all_gather | solution.py:80
  8.4 341.2 %reduce-scatter.2.cloned.1.call-start = ((), (), s32[]{:S(2)}) async-start(), calls=%async_computation.1 | async-start | bytes 2621440 | tf_op jit(solution)/shard_map/reduce_scatter | solution.py:60
  129.6 42.6 %copy-start.4 = (s32[1024]{0:T(1024)S(1)}, s32[1024]{0:T(1024)}, u32[]{:S(2)}) copy-start(s32[1024]{0:T(1024)} %param.16) | copy-start | bytes 12292
  129.6 48.8 %copy-start.1 = (s32[32768]{0:T(1024)S(1)}, s32[32768]{0:T(1024)}, u32[]{:S(2)}) copy-start(s32[32768]{0:T(1024)} %param.14) | copy-start | bytes 393220
  149.2 35.4 %copy-start.3 = (s32[32768]{0:T(1024)S(1)}, s32[32768]{0:T(1024)}, u32[]{:S(2)}) copy-start(s32[32768]{0:T(1024)} %param.15) | copy-start | bytes 393220
  149.2 41.6 %copy-start.2 = (f32[32768]{0:T(1024)S(1)}, f32[32768]{0:T(1024)}, u32[]{:S(2)}) copy-start(f32[32768]{0:T(1024)} %param.13) | copy-start | bytes 393220
  172.3 47.7 %copy-start.5 = (f32[1024]{0:T(1024)S(1)}, f32[1024]{0:T(1024)}, u32[]{:S(2)}) copy-start(f32[1024]{0:T(1024)} %param.17) | copy-start | bytes 12292
  327.0 173.4 %all-reduce.3.cloned.1.call-start = ((), (), s32[]{:S(2)}) async-start(), calls=%async_computation.2 | async-start | bytes 524288 | tf_op jit(solution)/shard_map/psum | solution.py:83
  352.3 170.2 %all-gather.7.cloned.1.call-start = ((), (), s32[]{:S(2)}) async-start(), calls=%async_computation.5 | async-start | bytes 1310720 | tf_op jit(solution)/shard_map/all_gather | solution.py:80
  352.9 318.9 %all-reduce.5.cloned.1.call-start = ((), (), s32[]{:S(2)}) async-start(), calls=%async_computation.3 | async-start | bytes 524288 | tf_op jit(solution)/shard_map/psum | solution.py:83
Sparse Core Ops, SparseCore 0:
  9.2 26.2 all-gather.4
  327.1 22.5 reduce-scatter.1
  353.6 146.7 all-reduce.2
  502.2 20.2 all-gather.6
  526.2 145.5 all-reduce.4
